TPU v7x, 32 devices: a whole 2x2x4 slice. The times are simulated.
32 devices in a mesh: dp: 8 (over y, x, core), mp: 4 (over z).
Axes of the slice: x: 2, y: 2, z: 4, core: 2. Of those that a mesh axis runs over, the one named last changes fastest.
Arguments:
- act_in: bfloat16 [1024, 4096], P('dp', 'mp'), may hold values from -6 to 6
- grad_in: bfloat16 [1024, 16384], P('dp'), may hold values from -6 to 6
- query_act: bfloat16 [1024, 4096], P('dp', 'mp'), may hold values from -6 to 6
- query_grad: bfloat16 [1024, 16384], P('dp'), may hold values from -6 to 6
- act_basis: bfloat16 [4096, 128], P('mp'), may hold values from -1.1 to 1.1
- grad_basis: bfloat16 [16384, 128], P('dp'), may hold values from -1.1 to 1.1
- seq_lengths: int32 [4], replicated, may hold values from 1 to 256, 768 in all
Outputs:
- moments: float32 [4096, 16384], P('mp', 'dp')
- scores: float32 [64, 4], replicated
Inputs may be any that keep to these rules, and one draw needn't show every extreme that they name: `seq_lengths`: live tokens are the first ones of each sequence, and one sequence is full.
All inputs are finite; a program needn't handle non-finite values.
Results may differ from a plain program's by a relative error of at most 0.0046.
Values may be sent and summed in bfloat16 or wider, within the bound.
A program may use at most 192 MiB of HBM per device.

v0:
```python
import math
import jax
import jax.numpy as jnp
from jax import lax
from jax.sharding import PartitionSpec as P

D = 4096
FF = 16384
QUERIES = 64
QUERY_LEN = 16
damping = 0.1


def rotate(rows_in, basis_rows):
    count_rows, full_width = rows_in.shape
    block_size = basis_rows.shape[1]
    blocks = full_width // block_size
    product = jnp.einsum(
        "nbk,bkc->nbc",
        rows_in.reshape(count_rows, blocks, block_size),
        basis_rows.reshape(blocks, block_size, block_size),
        preferred_element_type=jnp.float32,
    )
    return product.reshape(count_rows, full_width)


def local(act_in, grad_in, query_act, query_grad, act_basis, grad_basis, seq_lengths):
    dp_count = lax.axis_size("dp")
    dp_index = lax.axis_index("dp")
    tok_dev = act_in.shape[0]
    seq_count = seq_lengths.shape[0]
    total_tokens = tok_dev * dp_count
    seq_len = total_tokens // seq_count
    global_rows = dp_index * tok_dev + jnp.arange(tok_dev, dtype=jnp.int32)
    seq_index = global_rows // seq_len
    within = global_rows % seq_len
    matches = seq_index[:, None] == jnp.arange(seq_count, dtype=jnp.int32)[None, :]
    row_length = jnp.sum(jnp.where(matches, seq_lengths[None, :], 0), axis=1)
    live_rows = (within < row_length).astype(jnp.float32)
    act_rot = (rotate(act_in, act_basis) * live_rows[:, None]).astype(jnp.bfloat16)
    query_act_rot = rotate(query_act, act_basis).astype(jnp.bfloat16)
    gathered_act, gathered_query = (
        lax.all_gather(act_rot, "dp", axis=0, tiled=True),
        lax.all_gather(query_act_rot, "dp", axis=0, tiled=True),
    )
    grad_cols, query_cols = (
        lax.all_to_all(grad_in, "dp", split_axis=1, concat_axis=0, tiled=True),
        lax.all_to_all(query_grad, "dp", split_axis=1, concat_axis=0, tiled=True),
    )
    grad_rot = rotate(grad_cols, grad_basis).astype(jnp.bfloat16)
    query_grad_rot = rotate(query_cols, grad_basis).astype(jnp.bfloat16)
    act_square = jnp.square(gathered_act.astype(jnp.float32)).astype(jnp.bfloat16)
    grad_square = jnp.square(grad_rot.astype(jnp.float32)).astype(jnp.bfloat16)
    counted = jnp.sum(seq_lengths).astype(jnp.float32)
    moments = (
        jnp.einsum("ti,tj->ij", act_square, grad_square, preferred_element_type=jnp.float32)
        / counted
    )
    weights = 1.0 / (moments + damping)
    act_width = gathered_act.shape[1]
    grad_width = grad_rot.shape[1]
    seq_acts = gathered_act.reshape(seq_count, seq_len, act_width)
    seq_grads = grad_rot.reshape(seq_count, seq_len, grad_width)
    seq_grad = jnp.einsum("sli,slj->sij", seq_acts, seq_grads, preferred_element_type=jnp.float32)
    scale_seq = lax.rsqrt(seq_lengths.astype(jnp.float32))
    precond = (weights[None, :, :] * seq_grad * scale_seq[:, None, None]).astype(jnp.bfloat16)
    mapped = jnp.einsum("ui,sij->suj", gathered_query, precond, preferred_element_type=jnp.float32)
    per_row = jnp.sum(mapped * query_grad_rot.astype(jnp.float32)[None, :, :], axis=2)
    per_query = jnp.sum(per_row.reshape(seq_count, QUERIES, QUERY_LEN), axis=2)
    partial_scores = per_query.T / math.sqrt(QUERY_LEN * D * FF)
    scores = lax.psum(partial_scores, ("dp", "mp"))
    return (moments, scores)


def solution(mesh):
    return jax.shard_map(
        local,
        mesh=mesh,
        in_specs=(
            P("dp", "mp"),
            P("dp", None),
            P("dp", "mp"),
            P("dp", None),
            P("mp", None),
            P("dp", None),
            P(),
        ),
        out_specs=(P("mp", "dp"), P()),
        check_vma=False,
    )
```

profile of v0, /device:TPU:0, one launch (start us, length us, event | category | flops | bytes accessed | tf_op | source)
XLA Modules:
  0.0 238.3 jit_solution(18068171213799246787)
XLA Ops:
  7.2 0.0 copy-start
  7.2 4.8 %copy.93 = bf16[16,8,8,2048]{3,2,0,1:T(8,128)(2,1)} copy(bf16[16,8,8,2048]{3,2,1,0:T(8,128)(2,1)} %bitcast.72) | data formatting | bytes 8388608 | tf_op jit(solution)/shard_map/all_to_all | solution.py:47
  12.0 5.3 %all-to-all-start = ((bf16[128,8,2048]{2,0,1:T(8,128)(2,1)}), bf16[128,8,2048]{2,0,1:T(8,128)(2,1)}, u32[]{:S(2)}, u32[]{:S(2)}) async-start(bf16[128,8,2048]{2,0,1:T(8,128)(2,1)} %bitcast.68), calls=%async_computation | async-start | bytes 8388608 | tf_op jit(solution)/shard_map/all_to_all | solution.py:47
  17.4 0.0 all-gather.3.cloned.1.call-start
  17.4 0.0 copy-done.2
  17.4 0.3 fusion.15
  17.8 0.2 copy.44
  18.0 0.1 select_reduce_fusion
  18.1 0.8 multiply_convert_fusion.4
  18.9 0.0 all-gather.3.cloned.1.call-update
  18.9 4.7 %copy.92 = bf16[16,8,8,2048]{3,2,0,1:T(8,128)(2,1)} copy(bf16[16,8,8,2048]{3,2,1,0:T(8,128)(2,1)} %bitcast.73) | data formatting | bytes 8388608 | tf_op jit(solution)/shard_map/all_to_all | solution.py:48
  23.7 51.3 %all-to-all-done = bf16[128,8,2048]{2,0,1:T(8,128)(2,1)} async-done(((bf16[128,8,2048]{2,0,1:T(8,128)(2,1)}), bf16[128,8,2048]{2,0,1:T(8,128)(2,1)}, u32[]{:S(2)}, u32[]{:S(2)}) %all-to-all-start) | async-done | bytes 4194336 | tf_op jit(solution)/shard_map/all_to_all | solution.py:47
  74.9 4.7 %all-to-all-start.1 = ((bf16[128,8,2048]{2,0,1:T(8,128)(2,1)}), bf16[128,8,2048]{2,0,1:T(8,128)(2,1)}, u32[]{:S(2)}, u32[]{:S(2)}) async-start(bf16[128,8,2048]{2,0,1:T(8,128)(2,1)} %bitcast.69), calls=%async_computation.1 | async-start | bytes 8388608 | tf_op jit(solution)/shard_map/all_to_all | solution.py:48
  79.6 0.0 all-gather.5.cloned.1.call-start
  79.7 0.0 copy-done.3
  79.7 0.3 convolution_convert_fusion
  80.0 0.9 copy.52
  80.9 0.0 all-gather.5.cloned.1.call-update
  80.9 0.6 reduce_sum.37
  82.2 3.6 %copy.67 = bf16[128,8,16,128]{3,2,1,0:T(8,128)(2,1)S(1)} copy(bf16[128,8,16,128]{3,1,2,0:T(8,128)(2,1)} %bitcast.30) | data formatting | bytes 8388608
  85.8 0.0 copy-done
  85.8 5.9 %multiply_convert_fusion.1 = (bf16[16,128,1024]{2,1,0:T(8,128)(2,1)}, bf16[16,128,1024]{2,1,0:T(8,128)(2,1)}) fusion(bf16[16,128,128]{2,1,0:T(8,128)(2,1)S(1)} %bitcast.63, bf16[1024,16,128]{2,1,0:T(8,128)(2,1)S(1)} %bitcast.65), kind=kOutput, calls=%fused_computation.4 | convolution fusion | flops 545259520 | bytes 13107200 | tf_op jit(solution)/shard_map/nbk,bkc->nbc/dot_general | solution.py:18
  91.8 7.8 %convert_element_type.86 = bf16[4,256,2048]{1,0,2:T(4,128)(2,1)} reshape(bf16[1024,16,128]{0,2,1:T(8,128)(2,1)} %bitcast.66) | data formatting | bytes 8388608 | tf_op jit(solution)/shard_map/convert_element_type | solution.py:50
  99.6 37.5 %all-to-all-done.1 = bf16[128,8,2048]{2,0,1:T(8,128)(2,1)} async-done(((bf16[128,8,2048]{2,0,1:T(8,128)(2,1)}), bf16[128,8,2048]{2,0,1:T(8,128)(2,1)}, u32[]{:S(2)}, u32[]{:S(2)}) %all-to-all-start.1) | async-done | bytes 4194336 | tf_op jit(solution)/shard_map/all_to_all | solution.py:48
  137.1 3.6 %copy.68 = bf16[128,8,16,128]{3,2,1,0:T(8,128)(2,1)S(1)} copy(bf16[128,8,16,128]{3,1,2,0:T(8,128)(2,1)} %bitcast.34) | data formatting | bytes 8388608
  140.7 5.8 %convert_convert_fusion = f32[16,128,1024]{2,1,0:T(8,128)} fusion(bf16[16,128,128]{2,1,0:T(8,128)(2,1)S(1)} %bitcast.64, bf16[1024,16,128]{2,1,0:T(8,128)(2,1)S(1)} %bitcast.67), kind=kOutput, calls=%fused_computation.12 | convolution fusion | flops 541065216 | bytes 13107200 | tf_op jit(solution)/shard_map/nbk,bkc->nbc/dot_general | solution.py:18
  146.5 13.9 %add_divide_fusion = (f32[1024,2048]{1,0:T(8,128)}, f32[1024,2048]{1,0:T(8,128)}) fusion(f32[]{:T(128)S(6)} %convert_element_type.84, bf16[1024,2048]{0,1:T(8,128)(2,1)} %bitcast.71, bf16[1024,1024]{1,0:T(8,128)(2,1)} %all-gather.3.cloned.1.call-done), kind=kOutput, calls=%fused_computation.3 | convolution fusion | flops 4304404480 | bytes 23068676 | tf_op jit(solution)/shard_map/ti,tj->ij/dot_general | solution.py:56
  160.4 30.5 %fusion = f32[4,1024]{1,0:T(4,128)S(1)} fusion(f32[1024,2048]{0,1:T(8,128)} %bitcast.70, bf16[4,256,1024]{2,1,0:T(8,128)(2,1)S(1)} %bitcast.78, f32[4]{0:T(128)S(1)} %convert_rsqrt_fusion, f32[1024,2048]{1,0:T(8,128)} %get-tuple-element.4, bf16[4,256,2048]{1,0,2:T(4,128)(2,1)} %convert_element_type.86, bf16[1024,1024]{1,0:T(8,128)(2,1)} %all-gather.5.cloned.1.call-done), kind=kOutput, calls=%fused_computation.1 | convolution fusion | flops 21516775424 | bytes 25182224 | tf_op jit(solution)/shard_map/ui,sij->suj/dot_general | solution.py:67
  191.0 0.1 reshape.108
  191.1 0.1 reduce_sum.39
  191.2 40.3 %psum.7 = f32[64,4]{0,1:T(4,128)} all-reduce(f32[64,4]{0,1:T(4,128)S(1)} %multiply_bitcast_fusion), channel_id=1, replica_groups=mesh['dp'=8,'mp'=4] {'dp','mp'}, use_global_device_ids=true, to_apply=%region_4.5 | all-reduce | flops 256 | bytes 2048 | tf_op jit(solution)/shard_map/psum | solution.py:71
  231.5 0.0 copy-done.1
  (15 shorter events, 0.1 us)
Async XLA Ops:
  7.2 78.6 %copy-start = (bf16[2048,128]{1,0:T(8,128)(2,1)S(1)}, bf16[2048,128]{1,0:T(8,128)(2,1)}, u32[]{:S(2)}) copy-start(bf16[2048,128]{1,0:T(8,128)(2,1)} %param.12) | copy-start | bytes 1572868
  12.0 5.4 %copy-start.2 = (bf16[1024,128]{1,0:T(8,128)(2,1)S(1)}, bf16[1024,128]{1,0:T(8,128)(2,1)}, u32[]{:S(2)}) copy-start(bf16[1024,128]{1,0:T(8,128)(2,1)} %param.11) | copy-start | bytes 786436
  12.0 5.4 %copy-start.4 = (bf16[128,1024]{1,0:T(8,128)(2,1)S(1)}, bf16[128,1024]{1,0:T(8,128)(2,1)}, u32[]{:S(2)}) copy-start(bf16[128,1024]{1,0:T(8,128)(2,1)} %param.7) | copy-start | bytes 786436
  12.0 6.0 %copy-start.6 = (s32[4]{0:T(128)S(1)}, s32[4]{0:T(128)}, u32[]{:S(2)}) copy-start(s32[4]{0:T(128)} %param.13) | copy-start | bytes 52
  12.0 62.9 %all-to-all-start = ((bf16[128,8,2048]{2,0,1:T(8,128)(2,1)}), bf16[128,8,2048]{2,0,1:T(8,128)(2,1)}, u32[]{:S(2)}, u32[]{:S(2)}) async-start(bf16[128,8,2048]{2,0,1:T(8,128)(2,1)} %bitcast.68), calls=%async_computation | async-start | bytes 8388608 | tf_op jit(solution)/shard_map/all_to_all | solution.py:47
  17.4 129.2 %all-gather.3.cloned.1.call-start = ((), (), s32[]{:S(2)}) async-start(), calls=%async_computation.2 | async-start | bytes 2359296 | tf_op jit(solution)/shard_map/all_gather | solution.py:43
  74.9 4.8 %copy-start.3 = (bf16[128,1024]{1,0:T(8,128)(2,1)S(1)}, bf16[128,1024]{1,0:T(8,128)(2,1)}, u32[]{:S(2)}) copy-start(bf16[128,1024]{1,0:T(8,128)(2,1)} %param.9) | copy-start | bytes 786436
  74.9 62.2 %all-to-all-start.1 = ((bf16[128,8,2048]{2,0,1:T(8,128)(2,1)}), bf16[128,8,2048]{2,0,1:T(8,128)(2,1)}, u32[]{:S(2)}, u32[]{:S(2)}) async-start(bf16[128,8,2048]{2,0,1:T(8,128)(2,1)} %bitcast.69), calls=%async_computation.1 | async-start | bytes 8388608 | tf_op jit(solution)/shard_map/all_to_all | solution.py:48
  79.6 80.8 %all-gather.5.cloned.1.call-start = ((), (), s32[]{:S(2)}) async-start(), calls=%async_computation.3 | async-start | bytes 2359296 | tf_op jit(solution)/shard_map/all_gather | solution.py:44
  146.5 13.9 %copy-start.5 = (bf16[1024,1024]{1,0:T(8,128)(2,1)S(1)}, bf16[1024,1024]{1,0:T(8,128)(2,1)}, u32[]{:S(2)}) copy-start(bf16[1024,1024]{1,0:T(8,128)(2,1)} %all-gather.3.cloned.1.call-done) | copy-start | bytes 6291460
  160.4 71.1 %copy-start.1 = (bf16[2048,128]{1,0:T(8,128)(2,1)S(1)}, bf16[2048,128]{1,0:T(8,128)(2,1)}, u32[]{:S(2)}) copy-start(bf16[2048,128]{1,0:T(8,128)(2,1)} %param.12) | copy-start | bytes 1572868
Sparse Core Ops, SparseCore 0:
  20.1 49.0 all-gather.2
  82.4 48.9 all-gather.4
where the time goes:
time: 239 us; the launch traced here: 238 us
  waiting for transfers between devices  88.8 us (37%)
  matrix products  56.8 us (24%)
  blocking collectives  40.3 us (17%)
  local copies, waits for them, and re-layouts  25.7 us (11%)
  between operations  14.8 us (6%)
  starting transfers between devices  10.1 us (4%)
    all_to_all x1, waiting for transfers between devices, local(): lax.all_to_all(grad_in, 'dp', split_axis=1, concat_axis=0, tiled=True)  51.3 us
    psum x1, blocking collectives, local(): scores = lax.psum(partial_scores, ('dp', 'mp'))  40.3 us
    all_to_all x1, waiting for transfers between devices, local(): lax.all_to_all(query_grad, 'dp', split_axis=1, concat_axis=0, tiled=True)  37.5 us
    dot_general x1, matrix products, local(): jnp.einsum('ui,sij->suj', gathered_query, precond, preferred_element_type...  30.5 us
    dot_general x1, matrix products, local(): jnp.einsum('ti,tj->ij', act_square, grad_square, preferred_element_type=j...  13.9 us
    dot_general x4, matrix products, rotate(): jnp.einsum('nbk,bkc->nbc', rows_in.reshape(count_rows, blocks, block_size...  12.4 us
    convert_element_type x1, local copies, waits for them, and re-layouts, local(): grad_rot = rotate(grad_cols, grad_basis).astype(jnp.bfloat16)  7.83 us
    unnamed x16, local copies, waits for them, and re-layouts  7.19 us
  transfers between devices with their start and end apart: 4, of which 2 were waited for; matrix products, arithmetic and copies ran while one was open for 20% of the time, Pallas kernels for 0%

commit v1 on v0

--- a/solution.py
+++ b/solution.py
@@ -68,7 +68,8 @@
     per_row = jnp.sum(mapped * query_grad_rot.astype(jnp.float32)[None, :, :], axis=2)
     per_query = jnp.sum(per_row.reshape(seq_count, QUERIES, QUERY_LEN), axis=2)
     partial_scores = per_query.T / math.sqrt(QUERY_LEN * D * FF)
-    scores = lax.psum(partial_scores, ("dp", "mp"))
+    pieces = lax.all_gather(partial_scores, ("dp", "mp"), axis=0, tiled=False)
+    scores = pieces.sum(axis=0)
     return (moments, scores)
 
 

time: 239 us -> 267 us (1.12)
  blocking collectives: 40.3 us -> 67.6 us
    all_gather x0 -> x1, blocking collectives: none -> 67.6 us  [local(): pieces = lax.all_gather(partial_scores, ('dp', 'mp'), axis=0, tiled=False)]
    psum x1 -> x0, blocking collectives: 40.3 us -> none  [local(): scores = lax.psum(partial_scores, ('dp', 'mp'))]
  transfers between devices with their start and end apart: 4 -> 4, of which waited for: 2 -> 2; matrix products, arithmetic and copies ran while one was open for 20% -> 18% of each run, Pallas kernels for 0% -> 0%
where the time goes in v1:
time: 267 us; the launch traced here: 266 us
  waiting for transfers between devices  88.8 us (33%)
  blocking collectives  67.6 us (25%)
  matrix products  56.8 us (21%)
  local copies, waits for them, and re-layouts  25.7 us (10%)
  between operations  14.8 us (6%)
  starting transfers between devices  10.1 us (4%)
    all_gather x1, blocking collectives, local(): pieces = lax.all_gather(partial_scores, ('dp', 'mp'), axis=0, tiled=False)  67.6 us
    all_to_all x1, waiting for transfers between devices, local(): lax.all_to_all(grad_in, 'dp', split_axis=1, concat_axis=0, tiled=True)  51.3 us
    all_to_all x1, waiting for transfers between devices, local(): lax.all_to_all(query_grad, 'dp', split_axis=1, concat_axis=0, tiled=True)  37.5 us
    dot_general x1, matrix products, local(): jnp.einsum('ui,sij->suj', gathered_query, precond, preferred_element_type...  30.5 us
    dot_general x1, matrix products, local(): jnp.einsum('ti,tj->ij', act_square, grad_square, preferred_element_type=j...  13.9 us
    dot_general x4, matrix products, rotate(): jnp.einsum('nbk,bkc->nbc', rows_in.reshape(count_rows, blocks, block_size...  12.4 us
    convert_element_type x1, local copies, waits for them, and re-layouts, local(): grad_rot = rotate(grad_cols, grad_basis).astype(jnp.bfloat16)  7.83 us
    unnamed x16, local copies, waits for them, and re-layouts  7.19 us
  transfers between devices with their start and end apart: 4, of which 2 were waited for; matrix products, arithmetic and copies ran while one was open for 18% of the time, Pallas kernels for 0%

profile of v1, /device:TPU:0, one launch (start us, length us, event | category | flops | bytes accessed | tf_op | source)
XLA Modules:
  0.0 266.3 jit_solution(2300657935739975165)
XLA Ops:
  7.2 0.0 copy-start
  7.2 4.8 %copy.108 = bf16[16,8,8,2048]{3,2,0,1:T(8,128)(2,1)} copy(bf16[16,8,8,2048]{3,2,1,0:T(8,128)(2,1)} %bitcast.74) | data formatting | bytes 8388608 | tf_op jit(solution)/shard_map/all_to_all | solution.py:47
  12.0 5.3 %all-to-all-start = ((bf16[128,8,2048]{2,0,1:T(8,128)(2,1)}), bf16[128,8,2048]{2,0,1:T(8,128)(2,1)}, u32[]{:S(2)}, u32[]{:S(2)}) async-start(bf16[128,8,2048]{2,0,1:T(8,128)(2,1)} %bitcast.70), calls=%async_computation | async-start | bytes 8388608 | tf_op jit(solution)/shard_map/all_to_all | solution.py:47
  17.4 0.0 all-gather.5.cloned.1.call-start
  17.4 0.0 copy-done.2
  17.4 0.3 fusion.15
  17.8 0.2 copy.59
  18.0 0.1 select_reduce_fusion
  18.1 0.8 multiply_convert_fusion.4
  18.9 0.0 all-gather.5.cloned.1.call-update
  18.9 4.7 %copy.107 = bf16[16,8,8,2048]{3,2,0,1:T(8,128)(2,1)} copy(bf16[16,8,8,2048]{3,2,1,0:T(8,128)(2,1)} %bitcast.75) | data formatting | bytes 8388608 | tf_op jit(solution)/shard_map/all_to_all | solution.py:48
  23.7 51.3 %all-to-all-done = bf16[128,8,2048]{2,0,1:T(8,128)(2,1)} async-done(((bf16[128,8,2048]{2,0,1:T(8,128)(2,1)}), bf16[128,8,2048]{2,0,1:T(8,128)(2,1)}, u32[]{:S(2)}, u32[]{:S(2)}) %all-to-all-start) | async-done | bytes 4194336 | tf_op jit(solution)/shard_map/all_to_all | solution.py:47
  74.9 4.7 %all-to-all-start.1 = ((bf16[128,8,2048]{2,0,1:T(8,128)(2,1)}), bf16[128,8,2048]{2,0,1:T(8,128)(2,1)}, u32[]{:S(2)}, u32[]{:S(2)}) async-start(bf16[128,8,2048]{2,0,1:T(8,128)(2,1)} %bitcast.71), calls=%async_computation.1 | async-start | bytes 8388608 | tf_op jit(solution)/shard_map/all_to_all | solution.py:48
  79.6 0.0 all-gather.7.cloned.1.call-start
  79.7 0.0 copy-done.3
  79.7 0.3 convolution_convert_fusion
  80.0 0.9 copy.67
  80.9 0.0 all-gather.7.cloned.1.call-update
  80.9 0.6 reduce_sum.46
  82.2 3.6 %copy.82 = bf16[128,8,16,128]{3,2,1,0:T(8,128)(2,1)S(1)} copy(bf16[128,8,16,128]{3,1,2,0:T(8,128)(2,1)} %bitcast.32) | data formatting | bytes 8388608
  85.8 0.0 copy-done
  85.8 5.9 %multiply_convert_fusion.1 = (bf16[16,128,1024]{2,1,0:T(8,128)(2,1)}, bf16[16,128,1024]{2,1,0:T(8,128)(2,1)}) fusion(bf16[16,128,128]{2,1,0:T(8,128)(2,1)S(1)} %bitcast.65, bf16[1024,16,128]{2,1,0:T(8,128)(2,1)S(1)} %bitcast.67), kind=kOutput, calls=%fused_computation.4 | convolution fusion | flops 545259520 | bytes 13107200 | tf_op jit(solution)/shard_map/nbk,bkc->nbc/dot_general | solution.py:18
  91.8 7.8 %convert_element_type.86 = bf16[4,256,2048]{1,0,2:T(4,128)(2,1)} reshape(bf16[1024,16,128]{0,2,1:T(8,128)(2,1)} %bitcast.68) | data formatting | bytes 8388608 | tf_op jit(solution)/shard_map/convert_element_type | solution.py:50
  99.6 37.5 %all-to-all-done.1 = bf16[128,8,2048]{2,0,1:T(8,128)(2,1)} async-done(((bf16[128,8,2048]{2,0,1:T(8,128)(2,1)}), bf16[128,8,2048]{2,0,1:T(8,128)(2,1)}, u32[]{:S(2)}, u32[]{:S(2)}) %all-to-all-start.1) | async-done | bytes 4194336 | tf_op jit(solution)/shard_map/all_to_all | solution.py:48
  137.1 3.6 %copy.83 = bf16[128,8,16,128]{3,2,1,0:T(8,128)(2,1)S(1)} copy(bf16[128,8,16,128]{3,1,2,0:T(8,128)(2,1)} %bitcast.36) | data formatting | bytes 8388608
  140.7 5.8 %convert_convert_fusion = f32[16,128,1024]{2,1,0:T(8,128)} fusion(bf16[16,128,128]{2,1,0:T(8,128)(2,1)S(1)} %bitcast.66, bf16[1024,16,128]{2,1,0:T(8,128)(2,1)S(1)} %bitcast.69), kind=kOutput, calls=%fused_computation.12 | convolution fusion | flops 541065216 | bytes 13107200 | tf_op jit(solution)/shard_map/nbk,bkc->nbc/dot_general | solution.py:18
  146.5 13.9 %add_divide_fusion = (f32[1024,2048]{1,0:T(8,128)}, f32[1024,2048]{1,0:T(8,128)}) fusion(f32[]{:T(128)S(6)} %convert_element_type.84, bf16[1024,2048]{0,1:T(8,128)(2,1)} %bitcast.73, bf16[1024,1024]{1,0:T(8,128)(2,1)} %all-gather.5.cloned.1.call-done), kind=kOutput, calls=%fused_computation.3 | convolution fusion | flops 4304404480 | bytes 23068676 | tf_op jit(solution)/shard_map/ti,tj->ij/dot_general | solution.py:56
  160.4 30.5 %fusion = f32[4,1024]{1,0:T(4,128)S(1)} fusion(f32[1024,2048]{0,1:T(8,128)} %bitcast.72, bf16[4,256,1024]{2,1,0:T(8,128)(2,1)S(1)} %bitcast.80, f32[4]{0:T(128)S(1)} %convert_rsqrt_fusion, f32[1024,2048]{1,0:T(8,128)} %get-tuple-element.4, bf16[4,256,2048]{1,0,2:T(4,128)(2,1)} %convert_element_type.86, bf16[1024,1024]{1,0:T(8,128)(2,1)} %all-gather.7.cloned.1.call-done), kind=kOutput, calls=%fused_computation.1 | convolution fusion | flops 21516775424 | bytes 25182224 | tf_op jit(solution)/shard_map/ui,sij->suj/dot_general | solution.py:67
  191.0 0.1 reshape.108
  191.1 0.1 reduce_sum.48
  191.2 67.6 %all-gather.1 = f32[32,64,4]{1,2,0:T(4,128)S(1)} all-gather(f32[1,64,4]{1,2,0:T(4,128)S(1)} %multiply_bitcast_fusion), channel_id=2, replica_groups=mesh['dp'=8,'mp'=4] {'dp','mp'}, dimensions={0}, use_global_device_ids=true | all-gather | bytes 33792 | tf_op jit(solution)/shard_map/all_gather | solution.py:71
  258.8 0.6 reduce_sum.49
  (16 shorter events, 0.1 us)
Async XLA Ops:
  7.2 78.6 %copy-start = (bf16[2048,128]{1,0:T(8,128)(2,1)S(1)}, bf16[2048,128]{1,0:T(8,128)(2,1)}, u32[]{:S(2)}) copy-start(bf16[2048,128]{1,0:T(8,128)(2,1)} %param.12) | copy-start | bytes 1572868
  12.0 5.4 %copy-start.2 = (bf16[1024,128]{1,0:T(8,128)(2,1)S(1)}, bf16[1024,128]{1,0:T(8,128)(2,1)}, u32[]{:S(2)}) copy-start(bf16[1024,128]{1,0:T(8,128)(2,1)} %param.11) | copy-start | bytes 786436
  12.0 5.4 %copy-start.4 = (bf16[128,1024]{1,0:T(8,128)(2,1)S(1)}, bf16[128,1024]{1,0:T(8,128)(2,1)}, u32[]{:S(2)}) copy-start(bf16[128,1024]{1,0:T(8,128)(2,1)} %param.7) | copy-start | bytes 786436
  12.0 6.0 %copy-start.6 = (s32[4]{0:T(128)S(1)}, s32[4]{0:T(128)}, u32[]{:S(2)}) copy-start(s32[4]{0:T(128)} %param.13) | copy-start | bytes 52
  12.0 62.9 %all-to-all-start = ((bf16[128,8,2048]{2,0,1:T(8,128)(2,1)}), bf16[128,8,2048]{2,0,1:T(8,128)(2,1)}, u32[]{:S(2)}, u32[]{:S(2)}) async-start(bf16[128,8,2048]{2,0,1:T(8,128)(2,1)} %bitcast.70), calls=%async_computation | async-start | bytes 8388608 | tf_op jit(solution)/shard_map/all_to_all | solution.py:47
  17.4 129.2 %all-gather.5.cloned.1.call-start = ((), (), s32[]{:S(2)}) async-start(), calls=%async_computation.2 | async-start | bytes 2359296 | tf_op jit(solution)/shard_map/all_gather | solution.py:43
  74.9 4.8 %copy-start.3 = (bf16[128,1024]{1,0:T(8,128)(2,1)S(1)}, bf16[128,1024]{1,0:T(8,128)(2,1)}, u32[]{:S(2)}) copy-start(bf16[128,1024]{1,0:T(8,128)(2,1)} %param.9) | copy-start | bytes 786436
  74.9 62.2 %all-to-all-start.1 = ((bf16[128,8,2048]{2,0,1:T(8,128)(2,1)}), bf16[128,8,2048]{2,0,1:T(8,128)(2,1)}, u32[]{:S(2)}, u32[]{:S(2)}) async-start(bf16[128,8,2048]{2,0,1:T(8,128)(2,1)} %bitcast.71), calls=%async_computation.1 | async-start | bytes 8388608 | tf_op jit(solution)/shard_map/all_to_all | solution.py:48
  79.6 80.8 %all-gather.7.cloned.1.call-start = ((), (), s32[]{:S(2)}) async-start(), calls=%async_computation.3 | async-start | bytes 2359296 | tf_op jit(solution)/shard_map/all_gather | solution.py:44
  146.5 13.9 %copy-start.5 = (bf16[1024,1024]{1,0:T(8,128)(2,1)S(1)}, bf16[1024,1024]{1,0:T(8,128)(2,1)}, u32[]{:S(2)}) copy-start(bf16[1024,1024]{1,0:T(8,128)(2,1)} %all-gather.5.cloned.1.call-done) | copy-start | bytes 6291460
  160.4 99.0 %copy-start.1 = (bf16[2048,128]{1,0:T(8,128)(2,1)S(1)}, bf16[2048,128]{1,0:T(8,128)(2,1)}, u32[]{:S(2)}) copy-start(bf16[2048,128]{1,0:T(8,128)(2,1)} %param.12) | copy-start | bytes 1572868
Sparse Core Ops, SparseCore 0:
  20.1 49.0 all-gather.4
  82.4 48.9 all-gather.6
